TPU v7x, 32 devices: a whole 2x2x4 slice. The times are simulated.
32 devices in a mesh: grp: 2 (over y), rx: 4 (over z), tw: 2 (over x), fq: 2 (over core).
Axes of the slice: x: 2, y: 2, z: 4, core: 2. Of those that a mesh axis runs over, the one named last changes fastest.
Arguments:
- traces: bfloat16 [8, 256, 15360], P('tw', ('grp', 'rx')), parts along dimension 1, may hold values from -48 to 48
- src_index: int32 [8, 64], P('grp'), parts along dimension 0, may hold values from 0 to 127
- valid: int32 [8, 256], P(None, 'grp'), parts along dimension 1, may hold values from 0 to 1, as said below
Outputs:
- correlations: bfloat16 [256, 256, 512], P(('tw', 'fq'), ('grp', 'rx')), parts along dimension 1
There are 2 independent parts, one for each index of `grp`. A program takes and returns all parts, laid end to end along the dimension named above; each array names one. Nothing has to cross between parts.
Inputs may be any that keep to these rules, and one draw needn't show every extreme that they name: `valid`: some channels may be 0 in every window, and some windows 0 on every channel. `src_index`: A channel may be named by several sources.
All inputs are finite; a program needn't handle non-finite values.
Results may differ from a plain program's by a relative error of at most 0.0062.
Values may be sent and summed in bfloat16 or wider, within the bound.
No kernel may reach another device: no remote copies, remote signals or barrier semaphores. Data moves between devices by JAX's collectives and lax.ppermute only.
A program may use at most 128 MiB of HBM per device.

v0:
```python
import math
import jax
import jax.numpy as jnp
from jax import lax
from jax.sharding import PartitionSpec as P

NT = 15360
BAND = 512
F0 = 60
HW = 32
LAGS = 512
two_pi = 2.0 * math.pi
eps_power = 1e-05


def padded_2(block, sides, width):
    for axis, dim in sides:
        count = lax.axis_size(axis)
        forward = [(i, i + 1) for i in range(count - 1)]
        backward = [(target, source) for source, target in forward]
        low = lax.ppermute(
            lax.slice_in_dim(block, block.shape[dim] - width, None, axis=dim), axis, forward
        )
        high = lax.ppermute(lax.slice_in_dim(block, 0, width, axis=dim), axis, backward)
        block = jnp.concatenate([low, block, high], axis=dim)
    return block


def forward_block(row_count, bin_ids, period):
    sample_ids = lax.broadcasted_iota(jnp.int32, (row_count, 1, 1), 0)
    phase_index = sample_ids * bin_ids[None, :, :] % period
    angle_rad = phase_index.astype(jnp.float32) * (two_pi / period)
    coef_block = jnp.stack([jnp.cos(angle_rad), -jnp.sin(angle_rad)], axis=2)
    return coef_block.reshape(row_count, -1).astype(jnp.bfloat16)


def inverse_rows(bin_ids, lag_count, period):
    lag_shift = lax.broadcasted_iota(jnp.int32, (1, lag_count), 1) - lag_count // 2
    phase_index = bin_ids[..., None] * lag_shift % period
    angle_rad = phase_index.astype(jnp.float32) * (two_pi / period)
    return jnp.concatenate([jnp.cos(angle_rad), -jnp.sin(angle_rad)], axis=-2).astype(jnp.bfloat16)


def shards(traces, src_index, valid):
    win_count, chan_count, samples = traces.shape
    tw_count = lax.axis_size("tw")
    fq_count = lax.axis_size("fq")
    tw_pos = lax.axis_index("tw")
    fq_pos = lax.axis_index("fq")
    rx_pos = lax.axis_index("rx")
    band_share = BAND // fq_count
    narrow = band_share // tw_count
    block_len = 1024
    trace_rows = traces.reshape(win_count * chan_count, samples)
    local_bins = (
        F0
        + fq_pos * band_share
        + lax.broadcasted_iota(jnp.int32, (tw_count, narrow), 0) * narrow
        + lax.broadcasted_iota(jnp.int32, (tw_count, narrow), 1)
    )
    base_table = forward_block(block_len, local_bins, samples)

    def accumulate(turn_index, running):
        offset = turn_index * block_len
        trace_piece = lax.dynamic_slice_in_dim(trace_rows, offset, block_len, 1)
        partial_value = jnp.dot(trace_piece, base_table, preferred_element_type=jnp.float32)
        partial_value = partial_value.reshape(-1, tw_count, 2, narrow)
        part_real = partial_value[:, :, 0]
        part_imag = partial_value[:, :, 1]
        phase_index = offset * local_bins % samples
        angle_rad = phase_index.astype(jnp.float32) * (two_pi / samples)
        turn_real = jnp.cos(angle_rad)[None]
        turn_imag = -jnp.sin(angle_rad)[None]
        new_real = part_real * turn_real - part_imag * turn_imag
        new_imag = part_real * turn_imag + part_imag * turn_real
        return running + jnp.stack([new_real, new_imag], axis=2)

    spec_parts = lax.fori_loop(
        0,
        samples // block_len,
        accumulate,
        jnp.zeros((win_count * chan_count, tw_count, 2, narrow), jnp.float32),
    )
    bin_power = (
        spec_parts[:, :, 0] * spec_parts[:, :, 0] + spec_parts[:, :, 1] * spec_parts[:, :, 1]
    )
    bin_power = bin_power.reshape(-1, band_share)
    padded = padded_2(bin_power, (("fq", 1),), HW)
    row_ids = lax.broadcasted_iota(jnp.int32, (band_share + 2 * HW, band_share), 0)
    col_ids = lax.broadcasted_iota(jnp.int32, (band_share + 2 * HW, band_share), 1)
    box_matrix = ((row_ids - col_ids >= 0) & (row_ids - col_ids <= 2 * HW)).astype(jnp.float32)
    smooth = jnp.dot(
        padded, box_matrix, precision=lax.Precision.HIGHEST, preferred_element_type=jnp.float32
    ) / (2 * HW + 1)
    white_gain = lax.rsqrt(smooth + eps_power).reshape(-1, tw_count, 1, narrow)
    whitened = (
        (spec_parts * white_gain)
        .astype(jnp.bfloat16)
        .reshape(win_count, chan_count, tw_count, 2 * narrow)
    )
    valid_float = valid.astype(jnp.float32)
    source_ids = src_index.reshape(-1)
    src_total = source_ids.shape[0]
    channels_all = valid.shape[1]
    pick_all = (
        lax.broadcasted_iota(jnp.int32, (channels_all, src_total), 0) == source_ids[None, :]
    ).astype(jnp.float32)
    source_valid = jnp.dot(
        valid_float, pick_all, precision=lax.Precision.HIGHEST, preferred_element_type=jnp.float32
    )
    receiver_valid = lax.dynamic_slice_in_dim(valid_float, rx_pos * chan_count, chan_count, 1)
    pair_count = jnp.dot(
        source_valid.T,
        receiver_valid,
        precision=lax.Precision.HIGHEST,
        preferred_element_type=jnp.float32,
    )
    pair_floor = jnp.maximum(pair_count, 1.0)[:, :, None]
    pick_local = (
        source_ids[:, None]
        == rx_pos * chan_count + lax.broadcasted_iota(jnp.int32, (1, chan_count), 1)
    ).astype(jnp.bfloat16)
    inv_scale = 1.0 / math.sqrt(BAND)
    own_block = tw_pos * fq_count + fq_pos
    src_local = src_total // (tw_count * fq_count)
    local_terms = jnp.einsum(
        "sc,wcx->swx",
        pick_local,
        whitened.reshape(win_count, chan_count, tw_count * 2 * narrow),
        preferred_element_type=jnp.float32,
    )
    sources = lax.psum(local_terms.astype(jnp.bfloat16), "rx")
    own_sources = lax.all_to_all(
        sources[None], ("tw", "fq"), split_axis=1, concat_axis=0, tiled=True
    )
    all_windows = lax.all_gather(whitened[None], ("tw", "fq"), axis=0, tiled=True)
    src_valid_own = lax.dynamic_slice_in_dim(source_valid, own_block * src_local, src_local, 1)
    src_valid_own = jnp.transpose(src_valid_own.reshape(tw_count, win_count, src_local), (0, 2, 1))
    own_sources = own_sources.reshape(
        tw_count, fq_count, src_local, win_count, tw_count, 2, narrow
    ) * src_valid_own.reshape(tw_count, 1, src_local, win_count, 1, 1, 1).astype(jnp.bfloat16)
    all_windows = all_windows.reshape(
        tw_count, fq_count, win_count, chan_count, tw_count, 2, narrow
    ) * receiver_valid.reshape(tw_count, 1, win_count, chan_count, 1, 1, 1).astype(jnp.bfloat16)
    src_real = own_sources[..., 0, :]
    src_imag = own_sources[..., 1, :]
    rec_real = all_windows[..., 0, :]
    rec_imag = all_windows[..., 1, :]
    pattern = "tfswbx,tfwcbx->scfbx"
    cross_real = jnp.einsum(
        pattern, src_real, rec_real, preferred_element_type=jnp.float32
    ) + jnp.einsum(pattern, src_imag, rec_imag, preferred_element_type=jnp.float32)
    cross_imag = jnp.einsum(
        pattern, src_real, rec_imag, preferred_element_type=jnp.float32
    ) - jnp.einsum(pattern, src_imag, rec_real, preferred_element_type=jnp.float32)
    floor_own = lax.dynamic_slice_in_dim(pair_floor, own_block * src_local, src_local, 0)
    stacked = jnp.concatenate(
        [
            cross_real.reshape(src_local, chan_count, BAND),
            cross_imag.reshape(src_local, chan_count, BAND),
        ],
        axis=2,
    )
    stacked = (stacked / floor_own).astype(jnp.bfloat16)
    inv_table = inverse_rows(F0 + lax.broadcasted_iota(jnp.int32, (BAND,), 0), LAGS, NT)
    summed = jnp.dot(
        stacked.reshape(src_local * chan_count, 2 * BAND),
        inv_table,
        preferred_element_type=jnp.float32,
    ).reshape(src_local, chan_count, LAGS)
    return (summed * inv_scale).astype(jnp.bfloat16)


def solution(mesh):
    return jax.shard_map(
        shards,
        mesh=mesh,
        in_specs=(P("tw", ("grp", "rx"), None), P("grp", None), P(None, "grp")),
        out_specs=P(("tw", "fq"), ("grp", "rx"), None),
        check_vma=False,
    )
```

profile of v0, /device:TPU:0, one launch (start us, length us, event | category | flops | bytes accessed | tf_op | source)
XLA Modules:
  0.0 195.9 jit_solution(17614216192900421187)
XLA Ops:
  6.6 4.6 %cosine_convert_fusion.1 = (bf16[1024,2,1,128]{3,0,2,1:T(8,128)(2,1)S(1)}, bf16[1024,2,1,128]{3,0,2,1:T(8,128)(2,1)S(1)}) fusion(s32[2,128]{1,0:T(2,128)S(1)} %iota_add_fusion.2), kind=kLoop, calls=%fused_computation.47 | loop fusion | flops 3145728 | bytes 1049600 | tf_op jit(solution)/shard_map/convert.2
  11.3 0.5 copy.35
  11.8 0.5 copy.36
  12.4 34.7 %while.16 = (s32[]{:T(128)}, f32[128,2,2,128]{3,2,1,0:T(2,128)S(1)}, bf16[128,15360]{1,0:T(8,128)(2,1)}, bf16[1024,512]{1,0:T(8,128)(2,1)S(1)}, s32[2]{0:T(128)S...) while((s32[]{:T(128)}, f32[128,2,2,128]{3,2,1,0:T(2,128)S(1)}, ...), condition=%wide.region_1.2_spmd.clone, body=%wide.region_0.1_spmd.clone.sunk | while | flops 134613760 | bytes 3412133 | solution.py:78
  12.4 1.3 fusion.68
  14.0 0.3 multiply_subtract_fusion.2
  14.3 0.4 maximum_add_fusion.2
  14.7 1.3 fusion.68
  16.3 0.3 multiply_subtract_fusion.2
  16.6 0.4 maximum_add_fusion.2
  17.1 1.3 fusion.68
  18.6 0.3 multiply_subtract_fusion.2
  18.9 0.4 maximum_add_fusion.2
  19.4 1.3 fusion.68
  20.9 0.3 multiply_subtract_fusion.2
  21.2 0.4 maximum_add_fusion.2
  21.7 1.3 fusion.68
  23.3 0.3 multiply_subtract_fusion.2
  23.5 0.4 maximum_add_fusion.2
  24.0 1.3 fusion.68
  25.6 0.3 multiply_subtract_fusion.2
  25.9 0.4 maximum_add_fusion.2
  26.3 1.3 fusion.68
  28.2 0.4 maximum_add_fusion.2
  28.6 1.3 fusion.68
  30.5 0.4 maximum_add_fusion.2
  31.0 1.3 fusion.68
  32.8 0.4 maximum_add_fusion.2
  33.3 1.3 fusion.68
  35.1 0.4 maximum_add_fusion.2
  35.6 1.3 fusion.68
  37.4 0.4 maximum_add_fusion.2
  37.9 1.3 fusion.68
  39.8 0.4 maximum_add_fusion.2
  40.2 1.3 fusion.68
  42.1 0.4 maximum_add_fusion.2
  42.5 1.3 fusion.68
  44.4 0.4 maximum_add_fusion.2
  44.8 1.3 fusion.68
  46.7 0.4 maximum_add_fusion.2
  47.1 0.5 add_reduce_fusion
  47.8 2.4 %collective-permute-start = (f32[128,32]{1,0:T(8,128)S(1)}, f32[128,32]{1,0:T(8,128)S(1)}, u32[]{:S(2)}, u32[]{:S(2)}) collective-permute-start(f32[128,32]{1,0:T(8,128)S(1)} %get-tuple-element.179), channel_id=1, source_target_pairs={{0,1},{2,3},{4,5},{6,7},{8,9},{10,11},{12,13},{14,15},{16,17},{18,... | collective-permute-start | bytes 49160 | tf_op jit(solution)/shard_map/ppermute | solution.py:21
  50.2 1.3 collective-permute-start.1
  51.6 1.7 collective-permute-done.1
  53.3 0.3 fusion.16
  54.0 1.5 fusion.14
  55.7 0.3 fusion.49
  56.1 53.5 %all-reduce.2.cloned.1.call-done = bf16[1,256,4,512]{3,1,2,0:T(8,128)(2,1)} async-done(((bf16[1,256,4,512]{3,1,2,0:T(8,128)(2,1)}), bf16[1,256,4,512]{3,1,2,0:T(8,128)(2,1)}) %all-reduce.2.cloned.1.call-update) | async-done | bytes 1048592 | tf_op jit(solution)/shard_map/psum | solution.py:132
  109.7 3.0 %copy.40 = bf16[1,256,4,512]{3,2,0,1:T(4,128)(2,1)} copy(bf16[1,256,4,512]{3,1,2,0:T(8,128)(2,1)} %all-reduce.2.cloned.1.call-done) | data formatting | bytes 2097152 | tf_op jit(solution)/shard_map/psum | solution.py:132
  112.7 4.3 %all-to-all-start = ((bf16[1,256,4,512]{3,2,0,1:T(4,128)(2,1)}), bf16[1,256,4,512]{3,2,0,1:T(4,128)(2,1)}, u32[]{:S(2)}, u32[]{:S(2)}) async-start(bf16[1,256,4,512]{3,2,0,1:T(4,128)(2,1)} %copy.40), calls=%async_computation | async-start | bytes 2097152 | tf_op jit(solution)/shard_map/all_to_all | solution.py:133
  117.1 5.7 %cosine_convert_fusion = (bf16[512,512]{1,0:T(8,128)(2,1)}, bf16[512,512]{1,0:T(8,128)(2,1)}) fusion(s32[512]{0:T(512)S(1)} %get-tuple-element.185, s32[512]{0:T(512)S(1)} %get-tuple-element.186), kind=kLoop, calls=%fused_computation.40 | loop fusion | flops 3145728 | bytes 1052672 | tf_op jit(solution)/shard_map/convert
  123.0 12.0 %all_gather.3 = bf16[4,4,32,2,256]{4,2,3,1,0:T(8,128)(2,1)S(1)} all-gather(bf16[1,4,32,2,256]{4,2,3,1,0:T(8,128)(2,1)S(1)} %copy.38), channel_id=1, replica_groups=mesh['grp'=2,'rx'=4,'tw'=2,'fq'=2] {'tw','fq'}, dimensions={0}, use_global_device_ids=true | all-gather | bytes 655360 | tf_op jit(solution)/shard_map/all_gather | solution.py:136
  135.1 2.5 %copy.39 = bf16[2,2,4,32,2,2,128]{3,2,0,6,4,1,5:T(4,128)(2,1)} copy(bf16[2,2,4,32,2,2,128]{6,5,3,4,2,1,0:T(2,128)(2,1)S(1)} %reshape.161) | data formatting | bytes 1048576 | tf_op jit(solution)/shard_map/reshape | solution.py:142
  137.7 1.7 broadcast_multiply_fusion.1
  139.4 1.5 reshape.171
  140.9 4.3 %copy.42 = bf16[2,2,64,4,2,2,128]{2,3,0,6,4,1,5:T(4,128)(2,1)} copy(bf16[2,2,64,4,2,2,128]{6,5,4,3,2,1,0:T(2,128)(2,1)S(1)} %reshape.171) | data formatting | bytes 2097152 | tf_op jit(solution)/shard_map/reshape | solution.py:139
  145.1 1.7 broadcast_multiply_fusion
  146.9 1.8 fusion.29
  148.7 4.2 %fusion.30 = f32[2,2,128,32,64,1]{4,3,5,2,1,0:T(8,128)} fusion(bf16[2,2,64,4,2,2,128]{2,3,0,6,4,1,5:T(4,128)(2,1)S(1)} %bitcast.78, bf16[2,2,4,32,2,2,128]{3,2,0,6,4,1,5:T(4,128)(2,1)S(1)} %bitcast.74), kind=kOutput, calls=%fused_computation.54 | convolution fusion | flops 16777216 | bytes 6291456 | tf_op jit(solution)/shard_map/tfswbx,tfwcbx->scfbx/dot_general | solution.py:153
  152.9 4.3 %bitcast_add_fusion = f32[2,2,128,32,64]{4,3,2,1,0:T(8,128)} fusion(f32[2,2,128,32,64,1]{4,3,5,2,1,0:T(8,128)S(1)} %fusion.29, bf16[2,2,4,32,2,2,128]{3,2,0,6,4,1,5:T(4,128)(2,1)S(1)} %bitcast.75, bf16[2,2,64,4,2,2,128]{2,3,0,6,4,1,5:T(4,128)(2,1)S(1)} %bitcast.79), kind=kOutput, calls=%fused_computation.17 | convolution fusion | flops 17825792 | bytes 14680064 | tf_op jit(solution)/shard_map/tfswbx,tfwcbx->scfbx/dot_general | solution.py:152
  157.2 7.7 %copy.43 = f32[64,32,512]{2,1,0:T(8,128)} copy(f32[64,32,512]{0,1,2:T(8,128)} %bitcast.72) | data formatting | bytes 8388608 | tf_op jit(solution)/shard_map/concatenate | solution.py:157
  165.0 9.1 %bitcast_subtract_fusion = f32[2,2,128,32,64]{4,3,2,1,0:T(8,128)} fusion(f32[2,2,128,32,64,1]{4,3,5,2,1,0:T(8,128)} %fusion.30, bf16[2,2,4,32,2,2,128]{3,2,0,6,4,1,5:T(4,128)(2,1)S(1)} %bitcast.76, bf16[2,2,64,4,2,2,128]{2,3,0,6,4,1,5:T(4,128)(2,1)} %bitcast.80), kind=kOutput, calls=%fused_computation.16 | convolution fusion | flops 17825792 | bytes 14680064 | tf_op jit(solution)/shard_map/tfswbx,tfwcbx->scfbx/dot_general | solution.py:155
  174.0 7.8 %copy.44 = f32[64,32,512]{2,1,0:T(8,128)} copy(f32[64,32,512]{0,1,2:T(8,128)} %bitcast.71) | data formatting | bytes 8388608 | tf_op jit(solution)/shard_map/concatenate | solution.py:157
  181.8 7.2 %multiply_convert_fusion = bf16[64,32,512]{2,1,0:T(8,128)(2,1)} fusion(f32[64,32,512]{2,1,0:T(8,128)} %copy.44, f32[64,32,512]{2,1,0:T(8,128)} %copy.43, f32[64,32]{1,0:T(8,128)S(1)} %copy.45, bf16[512,512]{1,0:T(8,128)(2,1)S(1)} %copy-done.2, bf16[512,512]{1,0:T(8,128)(2,1)S(1)} %copy-done.1), kind=kOutput, calls=%fused_computation.18 | convolution fusion | flops 2157969408 | bytes 11542528 | tf_op jit(solution)/shard_map/dot_general | solution.py:166
  (74 shorter events, 8.2 us)
Async XLA Ops:
  6.5 103.1 %all-reduce.2.cloned.1.call-start = ((), (), s32[]{:S(2)}) async-start(), calls=%async_computation.1 | async-start | bytes 2097152 | tf_op jit(solution)/shard_map/psum | solution.py:132
  12.4 39.1 %copy-start.4 = (s32[4,64]{1,0:T(4,128)S(1)}, s32[4,64]{1,0:T(4,128)}, u32[]{:S(2)}) copy-start(s32[4,64]{1,0:T(4,128)} %param.6) | copy-start | bytes 3076
  47.7 7.8 %copy-start.3 = (s32[8,128]{1,0:T(8,128)S(1)}, s32[8,128]{1,0:T(8,128)}, u32[]{:S(2)}) copy-start(s32[8,128]{1,0:T(8,128)} %param.7) | copy-start | bytes 12292
  47.8 3.8 %collective-permute-start = (f32[128,32]{1,0:T(8,128)S(1)}, f32[128,32]{1,0:T(8,128)S(1)}, u32[]{:S(2)}, u32[]{:S(2)}) collective-permute-start(f32[128,32]{1,0:T(8,128)S(1)} %get-tuple-element.179), channel_id=1, source_target_pairs={{0,1},{2,3},{4,5},{6,7},{8,9},{10,11},{12,13},{14,15},{16,17},{18,... | collective-permute-start | bytes 49160 | tf_op jit(solution)/shard_map/ppermute | solution.py:21
  50.2 3.1 %collective-permute-start.1 = (f32[128,32]{1,0:T(8,128)S(1)}, f32[128,32]{1,0:T(8,128)S(1)}, u32[]{:S(2)}, u32[]{:S(2)}) collective-permute-start(f32[128,32]{1,0:T(8,128)S(1)} %get-tuple-element.180), channel_id=1, source_target_pairs={{1,0},{3,2},{5,4},{7,6},{9,8},{11,10},{13,12},{15,14},{17,16},{19,... | collective-permute-start | bytes 49160 | tf_op jit(solution)/shard_map/ppermute | solution.py:24
  112.7 26.7 %all-to-all-start = ((bf16[1,256,4,512]{3,2,0,1:T(4,128)(2,1)}), bf16[1,256,4,512]{3,2,0,1:T(4,128)(2,1)}, u32[]{:S(2)}, u32[]{:S(2)}) async-start(bf16[1,256,4,512]{3,2,0,1:T(4,128)(2,1)} %copy.40), calls=%async_computation | async-start | bytes 2097152 | tf_op jit(solution)/shard_map/all_to_all | solution.py:133
  146.9 6.0 %copy-start = (bf16[1,2,64,8,2,2,128]{2,3,0,6,4,1,5:T(8,128)(2,1)}, bf16[1,2,64,8,2,2,128]{2,3,0,6,4,1,5:T(8,128)(2,1)S(1)}, u32[]{:S(2)}) copy-start(bf16[1,2,64,8,2,2,128]{2,3,0,6,4,1,5:T(8,128)(2,1)S(1)} %broadcast_multiply_fusion) | copy-start | bytes 3145732
  174.0 7.8 %copy-start.1 = (bf16[512,512]{1,0:T(8,128)(2,1)S(1)}, bf16[512,512]{1,0:T(8,128)(2,1)}, u32[]{:S(2)}) copy-start(bf16[512,512]{1,0:T(8,128)(2,1)} %get-tuple-element.181) | copy-start | bytes 1572868
  174.0 7.8 %copy-start.2 = (bf16[512,512]{1,0:T(8,128)(2,1)S(1)}, bf16[512,512]{1,0:T(8,128)(2,1)}, u32[]{:S(2)}) copy-start(bf16[512,512]{1,0:T(8,128)(2,1)} %get-tuple-element.182) | copy-start | bytes 1572868
Sparse Core Ops, SparseCore 0:
  55.6 54.0 all-reduce.1
where the time goes:
time: 197 us; the launch traced here: 196 us
  waiting for transfers between devices  55.3 us (28%)
  matrix products  47.8 us (24%)
  local copies, waits for them, and re-layouts  31.2 us (16%)
  other arithmetic  27.4 us (14%)
  between operations  13.6 us (7%)
  blocking collectives  12 us (6%)
  starting transfers between devices  7.95 us (4%)
    psum x1, waiting for transfers between devices, shards(): sources = lax.psum(local_terms.astype(jnp.bfloat16), 'rx')  53.5 us
    dot_general x15, matrix products, accumulate(): jnp.dot(trace_piece, base_table, preferred_element_type=jnp.float32)  18.9 us
    concatenate x2, local copies, waits for them, and re-layouts, shards(): jnp.concatenate([cross_real.reshape(src_local, chan_count, BAND), cross_i...  15.5 us
    all_gather x1, blocking collectives, shards(): lax.all_gather(whitened[None], ('tw', 'fq'), axis=0, tiled=True)  12 us
    another operation x2, other arithmetic  10.3 us
    dot_general x1, matrix products, shards(): jnp.einsum(pattern, src_imag, rec_real, preferred_element_type=jnp.float32)  9.08 us
    dot_general x1, matrix products, shards(): jnp.dot(stacked.reshape(src_local * chan_count, 2 * BAND), inv_table, pre...  7.22 us
    add x15, other arithmetic, accumulate(): return running + jnp.stack([new_real, new_imag], axis=2)  6.72 us
  transfers between devices with their start and end apart: 4, of which 2 were waited for; matrix products, arithmetic and copies ran while one was open for 6% of the time, Pallas kernels for 0%

commit v1 on v0

--- a/solution.py
+++ b/solution.py
@@ -129,7 +129,7 @@
         whitened.reshape(win_count, chan_count, tw_count * 2 * narrow),
         preferred_element_type=jnp.float32,
     )
-    sources = lax.psum(local_terms.astype(jnp.bfloat16), "rx")
+    sources = jnp.sum(lax.all_gather(local_terms.astype(jnp.bfloat16), "rx"), axis=0)
     own_sources = lax.all_to_all(
         sources[None], ("tw", "fq"), split_axis=1, concat_axis=0, tiled=True
     )

time: 197 us -> 227 us (1.15)
  waiting for transfers between devices: 55.3 us -> 84.1 us
  other arithmetic: 27.4 us -> 30.4 us
    all_gather x0 -> x1, waiting for transfers between devices: none -> 82.3 us  [shards(): lax.all_gather(local_terms.astype(jnp.bfloat16), 'rx')]
    psum x1 -> x0, waiting for transfers between devices: 53.5 us -> none  [shards(): sources = lax.psum(local_terms.astype(jnp.bfloat16), 'rx')]
    reduce_sum x0 -> x1, other arithmetic: none -> 3.02 us  [shards(): jnp.sum(lax.all_gather(local_terms.astype(jnp.bfloat16), 'rx'), axis=0)]
    psum x1 -> x0, local copies, waits for them, and re-layouts: 3.01 us -> none  [shards(): sources = lax.psum(local_terms.astype(jnp.bfloat16), 'rx')]
  transfers between devices with their start and end apart: 4 -> 4, of which waited for: 2 -> 2; matrix products, arithmetic and copies ran while one was open for 6% -> 5% of each run, Pallas kernels for 0% -> 0%
where the time goes in v1:
time: 227 us; the launch traced here: 226 us
  waiting for transfers between devices  84.1 us (37%)
  matrix products  47.8 us (21%)
  other arithmetic  30.4 us (13%)
  local copies, waits for them, and re-layouts  30 us (13%)
  between operations  13.6 us (6%)
  blocking collectives  12 us (5%)
  starting transfers between devices  7.93 us (3%)
    all_gather x1, waiting for transfers between devices, shards(): lax.all_gather(local_terms.astype(jnp.bfloat16), 'rx')  82.3 us
    dot_general x15, matrix products, accumulate(): jnp.dot(trace_piece, base_table, preferred_element_type=jnp.float32)  18.9 us
    concatenate x2, local copies, waits for them, and re-layouts, shards(): jnp.concatenate([cross_real.reshape(src_local, chan_count, BAND), cross_i...  15.5 us
    all_gather x1, blocking collectives, shards(): lax.all_gather(whitened[None], ('tw', 'fq'), axis=0, tiled=True)  12 us
    another operation x2, other arithmetic  10.3 us
    dot_general x1, matrix products, shards(): jnp.einsum(pattern, src_imag, rec_real, preferred_element_type=jnp.float32)  9.08 us
    dot_general x1, matrix products, shards(): jnp.dot(stacked.reshape(src_local * chan_count, 2 * BAND), inv_table, pre...  7.22 us
    add x15, other arithmetic, accumulate(): return running + jnp.stack([new_real, new_imag], axis=2)  6.72 us
  transfers between devices with their start and end apart: 4, of which 2 were waited for; matrix products, arithmetic and copies ran while one was open for 5% of the time, Pallas kernels for 0%

profile of v1, /device:TPU:0, one launch (start us, length us, event | category | flops | bytes accessed | tf_op | source)
XLA Modules:
  0.0 226.5 jit_solution(16384148249282480802)
XLA Ops:
  6.6 4.6 %cosine_convert_fusion.1 = (bf16[1024,2,1,128]{3,0,2,1:T(8,128)(2,1)S(1)}, bf16[1024,2,1,128]{3,0,2,1:T(8,128)(2,1)S(1)}) fusion(s32[2,128]{1,0:T(2,128)S(1)} %iota_add_fusion.2), kind=kLoop, calls=%fused_computation.46 | loop fusion | flops 3145728 | bytes 1049600 | tf_op jit(solution)/shard_map/convert.3
  11.3 0.5 copy.43
  11.8 0.5 copy.44
  12.4 34.7 %while.16 = (s32[]{:T(128)}, f32[128,2,2,128]{3,2,1,0:T(2,128)S(1)}, bf16[128,15360]{1,0:T(8,128)(2,1)}, bf16[1024,512]{1,0:T(8,128)(2,1)S(1)}, s32[2]{0:T(128)S...) while((s32[]{:T(128)}, f32[128,2,2,128]{3,2,1,0:T(2,128)S(1)}, ...), condition=%wide.region_1.2_spmd.clone, body=%wide.region_0.1_spmd.clone.sunk | while | flops 134613760 | bytes 3412133 | solution.py:78
  12.4 1.3 fusion.67
  14.0 0.3 multiply_subtract_fusion.2
  14.3 0.4 maximum_add_fusion.2
  14.7 1.3 fusion.67
  16.3 0.3 multiply_subtract_fusion.2
  16.6 0.4 maximum_add_fusion.2
  17.1 1.3 fusion.67
  18.6 0.3 multiply_subtract_fusion.2
  18.9 0.4 maximum_add_fusion.2
  19.4 1.3 fusion.67
  20.9 0.3 multiply_subtract_fusion.2
  21.2 0.4 maximum_add_fusion.2
  21.7 1.3 fusion.67
  23.3 0.3 multiply_subtract_fusion.2
  23.5 0.4 maximum_add_fusion.2
  24.0 1.3 fusion.67
  25.9 0.4 maximum_add_fusion.2
  26.3 1.3 fusion.67
  28.2 0.4 maximum_add_fusion.2
  28.6 1.3 fusion.67
  30.5 0.4 maximum_add_fusion.2
  31.0 1.3 fusion.67
  32.8 0.4 maximum_add_fusion.2
  33.3 1.3 fusion.67
  35.1 0.4 maximum_add_fusion.2
  35.6 1.3 fusion.67
  37.4 0.4 maximum_add_fusion.2
  37.9 1.3 fusion.67
  39.8 0.4 maximum_add_fusion.2
  40.2 1.3 fusion.67
  42.1 0.4 maximum_add_fusion.2
  42.5 1.3 fusion.67
  44.4 0.4 maximum_add_fusion.2
  44.8 1.3 fusion.67
  46.7 0.4 maximum_add_fusion.2
  47.2 0.5 add_reduce_fusion
  47.8 2.4 %collective-permute-start = (f32[128,32]{1,0:T(8,128)S(1)}, f32[128,32]{1,0:T(8,128)S(1)}, u32[]{:S(2)}, u32[]{:S(2)}) collective-permute-start(f32[128,32]{1,0:T(8,128)S(1)} %get-tuple-element.179), channel_id=1, source_target_pairs={{0,1},{2,3},{4,5},{6,7},{8,9},{10,11},{12,13},{14,15},{16,17},{18,... | collective-permute-start | bytes 49160 | tf_op jit(solution)/shard_map/ppermute | solution.py:21
  50.2 1.3 collective-permute-start.1
  51.6 1.7 collective-permute-done.1
  53.3 0.3 fusion.15
  53.9 1.5 convolution_convert_fusion
  55.7 0.3 fusion.48
  56.1 82.3 %all-gather.3.cloned.1.call-done = bf16[1024,4,512]{2,0,1:T(8,128)(2,1)} async-done(((bf16[256,4,512]{2,0,1:T(8,128)(2,1)}), bf16[1024,4,512]{2,0,1:T(8,128)(2,1)}) %all-gather.3.cloned.1.call-update) | async-done | bytes 4194320 | tf_op jit(solution)/shard_map/all_gather | solution.py:132
  138.4 3.0 %reduce_sum.12 = bf16[256,4,512]{2,0,1:T(8,128)(2,1)S(1)} reduce(bf16[4,256,4,512]{3,1,0,2:T(8,128)(2,1)} %bitcast.83, bf16[]{:T(256)} %constant.125.clone.1), dimensions={0}, to_apply=%region_2.3 | reduce | flops 1572864 | bytes 5242882 | tf_op jit(solution)/shard_map/reduce_sum | solution.py:132
  141.5 1.8 copy.48
  143.3 4.2 %all-to-all-start = ((bf16[1,256,4,512]{3,2,0,1:T(4,128)(2,1)}), bf16[1,256,4,512]{3,2,0,1:T(4,128)(2,1)}, u32[]{:S(2)}, u32[]{:S(2)}) async-start(bf16[1,256,4,512]{3,2,0,1:T(4,128)(2,1)} %copy.48), calls=%async_computation | async-start | bytes 2097152 | tf_op jit(solution)/shard_map/all_to_all | solution.py:133
  147.7 5.7 %cosine_convert_fusion = (bf16[512,512]{1,0:T(8,128)(2,1)}, bf16[512,512]{1,0:T(8,128)(2,1)}) fusion(s32[512]{0:T(512)S(1)} %get-tuple-element.185, s32[512]{0:T(512)S(1)} %get-tuple-element.186), kind=kLoop, calls=%fused_computation.39 | loop fusion | flops 3145728 | bytes 1052672 | tf_op jit(solution)/shard_map/convert.1
  153.5 12.0 %all_gather.9 = bf16[4,4,32,2,256]{4,2,3,1,0:T(8,128)(2,1)S(1)} all-gather(bf16[1,4,32,2,256]{4,2,3,1,0:T(8,128)(2,1)S(1)} %copy.46), channel_id=1, replica_groups=mesh['grp'=2,'rx'=4,'tw'=2,'fq'=2] {'tw','fq'}, dimensions={0}, use_global_device_ids=true | all-gather | bytes 655360 | tf_op jit(solution)/shard_map/all_gather | solution.py:136
  165.7 2.5 %copy.47 = bf16[2,2,4,32,2,2,128]{3,2,0,6,4,1,5:T(4,128)(2,1)} copy(bf16[2,2,4,32,2,2,128]{6,5,3,4,2,1,0:T(2,128)(2,1)S(1)} %reshape.161) | data formatting | bytes 1048576 | tf_op jit(solution)/shard_map/reshape | solution.py:142
  168.3 1.7 broadcast_multiply_fusion.1
  170.0 1.5 reshape.172
  171.5 4.3 %copy.50 = bf16[2,2,64,4,2,2,128]{2,3,0,6,4,1,5:T(4,128)(2,1)} copy(bf16[2,2,64,4,2,2,128]{6,5,4,3,2,1,0:T(2,128)(2,1)S(1)} %reshape.172) | data formatting | bytes 2097152 | tf_op jit(solution)/shard_map/reshape | solution.py:139
  175.7 1.7 broadcast_multiply_fusion
  177.5 1.8 fusion.28
  179.2 4.2 %fusion.29 = f32[2,2,128,32,64,1]{4,3,5,2,1,0:T(8,128)} fusion(bf16[2,2,64,4,2,2,128]{2,3,0,6,4,1,5:T(4,128)(2,1)S(1)} %bitcast.78, bf16[2,2,4,32,2,2,128]{3,2,0,6,4,1,5:T(4,128)(2,1)S(1)} %bitcast.74), kind=kOutput, calls=%fused_computation.53 | convolution fusion | flops 16777216 | bytes 6291456 | tf_op jit(solution)/shard_map/tfswbx,tfwcbx->scfbx/dot_general | solution.py:153
  183.5 4.3 %bitcast_add_fusion = f32[2,2,128,32,64]{4,3,2,1,0:T(8,128)} fusion(f32[2,2,128,32,64,1]{4,3,5,2,1,0:T(8,128)S(1)} %fusion.28, bf16[2,2,4,32,2,2,128]{3,2,0,6,4,1,5:T(4,128)(2,1)S(1)} %bitcast.75, bf16[2,2,64,4,2,2,128]{2,3,0,6,4,1,5:T(4,128)(2,1)S(1)} %bitcast.79), kind=kOutput, calls=%fused_computation.17 | convolution fusion | flops 17825792 | bytes 14680064 | tf_op jit(solution)/shard_map/tfswbx,tfwcbx->scfbx/dot_general | solution.py:152
  187.8 7.7 %copy.51 = f32[64,32,512]{2,1,0:T(8,128)} copy(f32[64,32,512]{0,1,2:T(8,128)} %bitcast.72) | data formatting | bytes 8388608 | tf_op jit(solution)/shard_map/concatenate | solution.py:157
  195.5 9.1 %bitcast_subtract_fusion = f32[2,2,128,32,64]{4,3,2,1,0:T(8,128)} fusion(f32[2,2,128,32,64,1]{4,3,5,2,1,0:T(8,128)} %fusion.29, bf16[2,2,4,32,2,2,128]{3,2,0,6,4,1,5:T(4,128)(2,1)S(1)} %bitcast.76, bf16[2,2,64,4,2,2,128]{2,3,0,6,4,1,5:T(4,128)(2,1)} %bitcast.80), kind=kOutput, calls=%fused_computation.16 | convolution fusion | flops 17825792 | bytes 14680064 | tf_op jit(solution)/shard_map/tfswbx,tfwcbx->scfbx/dot_general | solution.py:155
  204.6 7.8 %copy.52 = f32[64,32,512]{2,1,0:T(8,128)} copy(f32[64,32,512]{0,1,2:T(8,128)} %bitcast.71) | data formatting | bytes 8388608 | tf_op jit(solution)/shard_map/concatenate | solution.py:157
  212.4 7.2 %multiply_convert_fusion = bf16[64,32,512]{2,1,0:T(8,128)(2,1)} fusion(f32[64,32,512]{2,1,0:T(8,128)} %copy.52, f32[64,32,512]{2,1,0:T(8,128)} %copy.51, f32[64,32]{1,0:T(8,128)S(1)} %copy.53, bf16[512,512]{1,0:T(8,128)(2,1)S(1)} %copy-done.2, bf16[512,512]{1,0:T(8,128)(2,1)S(1)} %copy-done.1), kind=kOutput, calls=%fused_computation.18 | convolution fusion | flops 2157969408 | bytes 11542528 | tf_op jit(solution)/shard_map/dot_general | solution.py:166
  (75 shorter events, 8.5 us)
Async XLA Ops:
  6.5 131.9 %all-gather.3.cloned.1.call-start = ((), (), s32[]{:S(2)}) async-start(), calls=%async_computation.1 | async-start | bytes 5242880 | tf_op jit(solution)/shard_map/all_gather | solution.py:132
  12.4 39.1 %copy-start.4 = (s32[4,64]{1,0:T(4,128)S(1)}, s32[4,64]{1,0:T(4,128)}, u32[]{:S(2)}) copy-start(s32[4,64]{1,0:T(4,128)} %param.6) | copy-start | bytes 3076
  47.1 8.3 %copy-start.3 = (s32[8,128]{1,0:T(8,128)S(1)}, s32[8,128]{1,0:T(8,128)}, u32[]{:S(2)}) copy-start(s32[8,128]{1,0:T(8,128)} %param.7) | copy-start | bytes 12292
  47.8 3.8 %collective-permute-start = (f32[128,32]{1,0:T(8,128)S(1)}, f32[128,32]{1,0:T(8,128)S(1)}, u32[]{:S(2)}, u32[]{:S(2)}) collective-permute-start(f32[128,32]{1,0:T(8,128)S(1)} %get-tuple-element.179), channel_id=1, source_target_pairs={{0,1},{2,3},{4,5},{6,7},{8,9},{10,11},{12,13},{14,15},{16,17},{18,... | collective-permute-start | bytes 49160 | tf_op jit(solution)/shard_map/ppermute | solution.py:21
  50.2 3.1 %collective-permute-start.1 = (f32[128,32]{1,0:T(8,128)S(1)}, f32[128,32]{1,0:T(8,128)S(1)}, u32[]{:S(2)}, u32[]{:S(2)}) collective-permute-start(f32[128,32]{1,0:T(8,128)S(1)} %get-tuple-element.180), channel_id=1, source_target_pairs={{1,0},{3,2},{5,4},{7,6},{9,8},{11,10},{13,12},{15,14},{17,16},{19,... | collective-permute-start | bytes 49160 | tf_op jit(solution)/shard_map/ppermute | solution.py:24
  143.3 26.7 %all-to-all-start = ((bf16[1,256,4,512]{3,2,0,1:T(4,128)(2,1)}), bf16[1,256,4,512]{3,2,0,1:T(4,128)(2,1)}, u32[]{:S(2)}, u32[]{:S(2)}) async-start(bf16[1,256,4,512]{3,2,0,1:T(4,128)(2,1)} %copy.48), calls=%async_computation | async-start | bytes 2097152 | tf_op jit(solution)/shard_map/all_to_all | solution.py:133
  177.5 6.0 %copy-start = (bf16[1,2,64,8,2,2,128]{2,3,0,6,4,1,5:T(8,128)(2,1)}, bf16[1,2,64,8,2,2,128]{2,3,0,6,4,1,5:T(8,128)(2,1)S(1)}, u32[]{:S(2)}) copy-start(bf16[1,2,64,8,2,2,128]{2,3,0,6,4,1,5:T(8,128)(2,1)S(1)} %broadcast_multiply_fusion) | copy-start | bytes 3145732
  204.6 7.8 %copy-start.1 = (bf16[512,512]{1,0:T(8,128)(2,1)S(1)}, bf16[512,512]{1,0:T(8,128)(2,1)}, u32[]{:S(2)}) copy-start(bf16[512,512]{1,0:T(8,128)(2,1)} %get-tuple-element.181) | copy-start | bytes 1572868
  204.6 7.8 %copy-start.2 = (bf16[512,512]{1,0:T(8,128)(2,1)S(1)}, bf16[512,512]{1,0:T(8,128)(2,1)}, u32[]{:S(2)}) copy-start(bf16[512,512]{1,0:T(8,128)(2,1)} %get-tuple-element.182) | copy-start | bytes 1572868
Sparse Core Ops, SparseCore 0:
  55.6 82.7 all-gather.2
